TPU v7x, 32 devices: a whole 2x2x4 slice. The times are simulated.
32 devices in a mesh: ladder: 4 (over x, core), space: 8 (over z, y).
Axes of the slice: x: 2, y: 2, z: 4, core: 2. Of those that a mesh axis runs over, the one named last changes fastest.
Arguments:
- initial: float32 [4, 256, 2048], P('ladder', 'space'), may hold values from -1.2 to 1.2
- mobility: float32 [256, 2048], P('space'), may hold values from 0.1 to 0.5
- tilt: float32 [256, 2048], P('space'), may hold values from -0.5 to 0.5
- drift: float32 [2048], replicated, may hold values from -0.6 to 0.6
- mix_weights: float32 [4, 2], P('ladder'), may hold values from 0.2 to 0.4
Outputs:
- path: float32 [4, 256, 2048], P('ladder', 'space')
All inputs are finite; a program needn't handle non-finite values.
Results may differ from a plain program's by a relative error of at most 0.00002.
Values sent between devices are 32-bit elements; how exact they have to be, the bound alone decides.
A program may use at most 64 MiB of HBM per device.

v0:
```python
import jax
import jax.numpy as jnp
from jax import lax
from jax.sharding import PartitionSpec as P

CYCLES = 2


def with_halo(cells, sides, width, closed):
    for axis, dim in sides:
        count = lax.axis_size(axis)
        ends = count if closed else count - 1
        head = lax.slice_in_dim(cells, 0, width, axis=dim)
        tail = lax.slice_in_dim(cells, cells.shape[dim] - width, cells.shape[dim], axis=dim)
        cells = jnp.concatenate(
            [
                lax.ppermute(tail, axis, [(i, (i + 1) % count) for i in range(ends)]),
                cells,
                lax.ppermute(head, axis, [((i + 1) % count, i) for i in range(ends)]),
            ],
            axis=dim,
        )
    return cells


def advance(field, mobility, tilt, rising, falling):
    below = jnp.roll(field, 1, -2)
    above = jnp.roll(field, -1, -2)
    vertical = below + above
    horizontal = jnp.roll(field, 1, -1) + jnp.roll(field, -1, -1)
    laplace = vertical + horizontal - 4.0 * field
    transport = rising * (field - below) + falling * (above - field)
    return field + 0.1 * mobility * (laplace + field - field * field * field + tilt) - transport


def body(initial, mobility, tilt, drift, mix_weights):
    depth = 12
    height = initial.shape[1]
    coeffs = with_halo(jnp.stack([mobility, tilt]), (("space", 1),), depth, True)
    mob_rim = coeffs[0]
    tilt_rim = coeffs[1]
    rising = jnp.maximum(drift, 0.0)[None, :]
    falling = jnp.minimum(drift, 0.0)[None, :]
    field = initial[0]
    lower_w = mix_weights[0, 0]
    upper_w = mix_weights[0, 1]
    count = lax.axis_size("ladder")
    place = lax.axis_index("ladder")
    for cycle in range(CYCLES):
        extended = with_halo(field, (("space", 0),), depth, True)
        for inner in range(depth):
            extended = advance(extended, mob_rim, tilt_rim, rising, falling)
        field = extended[depth : depth + height]
        beside = with_halo(field[None], (("ladder", 0),), 1, False)
        lower = jnp.where(place == 0, field, beside[0])
        upper = jnp.where(place == count - 1, field, beside[2])
        field = (1.0 - lower_w - upper_w) * field + lower_w * lower + upper_w * upper
    return field[None]


def solution(mesh):
    in_specs = (
        P("ladder", "space", None),
        P("space", None),
        P("space", None),
        P(),
        P("ladder", None),
    )
    out_specs = P("ladder", "space", None)
    return jax.shard_map(body, mesh=mesh, in_specs=in_specs, out_specs=out_specs, check_vma=False)
```

profile of v0, /device:TPU:1, one launch (start us, length us, event | category | flops | bytes accessed | tf_op | source)
XLA Modules:
  0.0 77.5 jit_solution(12381511379719850997)
XLA Ops:
  0.0 1.2 %fusion.199 = (f32[2,12,2048]{2,1,0:T(8,128)S(1)}, f32[2,12,2048]{2,1,0:T(8,128)S(1)}) fusion(f32[1,32,2048]{2,1,0:T(8,128)} %bitcast.141, f32[1,32,2048]{2,1,0:T(8,128)} %bitcast.143), kind=kLoop, calls=%fused_computation.308 | loop fusion | flops 98304 | bytes 917504 | tf_op jit(solution)/shard_map/stack | solution.py:39
  1.2 2.1 %collective-permute-start.2 = (f32[2,12,2048]{2,1,0:T(8,128)S(1)}, f32[2,12,2048]{2,1,0:T(8,128)S(1)}, u32[]{:S(2)}, u32[]{:S(2)}) collective-permute-start(f32[2,12,2048]{2,1,0:T(8,128)S(1)} %get-tuple-element.11), channel_id=1, source_target_pairs={{0,1},{1,2},{2,3},{3,4},{4,5},{5,6},{6,7},{7,0},{8,9},{9,10},{10,1... | collective-permute-start | bytes 589832 | tf_op jit(solution)/shard_map/ppermute | solution.py:17
  3.3 3.1 %collective-permute-start.3 = (f32[2,12,2048]{2,1,0:T(8,128)S(1)}, f32[2,12,2048]{2,1,0:T(8,128)S(1)}, u32[]{:S(2)}, u32[]{:S(2)}) collective-permute-start(f32[2,12,2048]{2,1,0:T(8,128)S(1)} %get-tuple-element.12), channel_id=1, source_target_pairs={{1,0},{2,1},{3,2},{4,3},{5,4},{6,5},{7,6},{0,7},{9,8},{10,9},{11,1... | collective-permute-start | bytes 589832 | tf_op jit(solution)/shard_map/ppermute | solution.py:19
  6.5 4.1 %collective-permute-start.1 = (f32[12,2048]{1,0:T(8,128)S(1)}, f32[12,2048]{1,0:T(8,128)S(1)}, u32[]{:S(2)}, u32[]{:S(2)}) collective-permute-start(f32[12,2048]{1,0:T(8,128)S(1)} %get-tuple-element.204), channel_id=1, source_target_pairs={{1,0},{2,1},{3,2},{4,3},{5,4},{6,5},{7,6},{0,7},{9,8},{10,9},{11,1... | collective-permute-start | bytes 294920 | tf_op jit(solution)/shard_map/ppermute | solution.py:19
  10.6 8.9 %collective-permute-done = f32[12,2048]{1,0:T(8,128)S(1)} collective-permute-done((f32[12,2048]{1,0:T(8,128)S(1)}, f32[12,2048]{1,0:T(8,128)S(1)}, u32[]{:S(2)}, u32[]{:S(2)}) %collective-permute-start) | collective-permute-done | bytes 98336 | tf_op jit(solution)/shard_map/ppermute | solution.py:17
  19.5 1.9 %collective-permute-done.1 = f32[12,2048]{1,0:T(8,128)S(1)} collective-permute-done((f32[12,2048]{1,0:T(8,128)S(1)}, f32[12,2048]{1,0:T(8,128)S(1)}, u32[]{:S(2)}, u32[]{:S(2)}) %collective-permute-start.1) | collective-permute-done | bytes 98336 | tf_op jit(solution)/shard_map/ppermute | solution.py:19
  21.9 0.6 copy-done.1
  22.8 0.6 slice-done
  23.4 0.5 fusion.10
  24.2 0.4 fusion.15
  25.0 0.4 fusion.20
  25.8 0.4 fusion.25
  26.6 0.4 fusion.30
  27.4 0.4 fusion.35
  31.5 0.5 fusion.219
  32.9 4.8 %collective-permute-start.4 = (f32[1,32,2048]{2,1,0:T(8,128)S(1)}, f32[1,32,2048]{2,1,0:T(8,128)S(1)}, u32[]{:S(2)}, u32[]{:S(2)}) collective-permute-start(f32[1,32,2048]{2,1,0:T(8,128)S(1)} %bitcast.145), channel_id=1, source_target_pairs={{0,8},{8,16},{16,24},{1,9},{9,17},{17,25},{2,10},{10,18},{18,26},{... | collective-permute-start | bytes 786440 | tf_op jit(solution)/shard_map/ppermute | solution.py:17
  37.7 1.9 %collective-permute-start.5 = (f32[1,32,2048]{2,1,0:T(8,128)S(1)}, f32[1,32,2048]{2,1,0:T(8,128)S(1)}, u32[]{:S(2)}, u32[]{:S(2)}) collective-permute-start(f32[1,32,2048]{2,1,0:T(8,128)S(1)} %bitcast.146), channel_id=1, source_target_pairs={{8,0},{16,8},{24,16},{9,1},{17,9},{25,17},{10,2},{18,10},{26,18},{... | collective-permute-start | bytes 786440 | tf_op jit(solution)/shard_map/ppermute | solution.py:19
  39.7 0.6 copy-done.7
  40.3 0.6 fusion.316
  42.1 3.3 %collective-permute-done.5 = f32[1,32,2048]{2,1,0:T(8,128)S(1)} collective-permute-done((f32[1,32,2048]{2,1,0:T(8,128)S(1)}, f32[1,32,2048]{2,1,0:T(8,128)S(1)}, u32[]{:S(2)}, u32[]{:S(2)}) %collective-permute-start.5) | collective-permute-done | bytes 262176 | tf_op jit(solution)/shard_map/ppermute | solution.py:19
  45.4 1.3 %fusion.214 = f32[32,2048]{1,0:T(8,128)S(1)} fusion(f32[32,2048]{1,0:T(8,128)S(1)} %fusion.195, f32[1,32,2048]{2,1,0:T(8,128)S(1)} %collective-permute-done.5, f32[1,32,2048]{2,1,0:T(8,128)S(1)} %collective-permute-done.4, f32[]{:T(128)} %bitcast.1, f32[]{:T(128)} %bitcast, f32[]{:T(128)S(6)} %sub.369, pred[]{:T(512)S(6)} %eq.9, pred[]{:T(512)S(6)} %eq.8), kind=kLoop, calls=%fused_computation.331 | loop fusion | flops 458752 | bytes 1048590 | tf_op jit(solution)/shard_map/add | solution.py:57
  47.1 3.9 %collective-permute-start.7 = (f32[12,2048]{1,0:T(8,128)S(1)}, f32[12,2048]{1,0:T(8,128)S(1)}, u32[]{:S(2)}, u32[]{:S(2)}) collective-permute-start(f32[12,2048]{1,0:T(8,128)S(1)} %get-tuple-element.202), channel_id=1, source_target_pairs={{1,0},{2,1},{3,2},{4,3},{5,4},{6,5},{7,6},{0,7},{9,8},{10,9},{11,1... | collective-permute-start | bytes 294920 | tf_op jit(solution)/shard_map/ppermute | solution.py:19
  50.9 2.4 %collective-permute-done.6 = f32[12,2048]{1,0:T(8,128)S(1)} collective-permute-done((f32[12,2048]{1,0:T(8,128)S(1)}, f32[12,2048]{1,0:T(8,128)S(1)}, u32[]{:S(2)}, u32[]{:S(2)}) %collective-permute-start.6) | collective-permute-done | bytes 98336 | tf_op jit(solution)/shard_map/ppermute | solution.py:17
  53.9 0.7 slice-done.1
  54.6 1.4 %fusion.65 = f32[56,2048]{1,0:T(8,128)S(1)} fusion(f32[56,2047]{1,0:T(8,128)S(1)} %get-tuple-element.104, f32[56,1]{1,0:T(8,128)S(1)} %get-tuple-element.106, f32[56,1]{1,0:T(8,128)S(1)} %get-tuple-element.105, f32[56,2047]{1,0:T(8,128)S(1)} %get-tuple-element.103, f32[1,2048]{1,0:T(1,128)S(1)} %slice-done.1, f32[55,2048]{1,0:T(8,128)S(1)} %get-tuple-element.102, ...), kind=kLoop, calls=%fused_computation.98 | loop fusion | flops 2867200 | bytes 3686400 | tf_op jit(solution)/shard_map/sub | solution.py:33
  61.2 0.4 fusion.100
  63.6 0.5 fusion.217
  64.9 2.9 %collective-permute-start.8 = (f32[1,32,2048]{2,1,0:T(8,128)S(1)}, f32[1,32,2048]{2,1,0:T(8,128)S(1)}, u32[]{:S(2)}, u32[]{:S(2)}) collective-permute-start(f32[1,32,2048]{2,1,0:T(8,128)S(1)} %bitcast.147), channel_id=1, source_target_pairs={{0,8},{8,16},{16,24},{1,9},{9,17},{17,25},{2,10},{10,18},{18,26},{... | collective-permute-start | bytes 786440 | tf_op jit(solution)/shard_map/ppermute | solution.py:17
  67.9 1.9 %collective-permute-start.9 = (f32[1,32,2048]{2,1,0:T(8,128)S(1)}, f32[1,32,2048]{2,1,0:T(8,128)S(1)}, u32[]{:S(2)}, u32[]{:S(2)}) collective-permute-start(f32[1,32,2048]{2,1,0:T(8,128)S(1)} %bitcast.148), channel_id=1, source_target_pairs={{8,0},{16,8},{24,16},{9,1},{17,9},{25,17},{10,2},{18,10},{26,18},{... | collective-permute-start | bytes 786440 | tf_op jit(solution)/shard_map/ppermute | solution.py:19
  69.8 1.4 %collective-permute-done.8 = f32[1,32,2048]{2,1,0:T(8,128)S(1)} collective-permute-done((f32[1,32,2048]{2,1,0:T(8,128)S(1)}, f32[1,32,2048]{2,1,0:T(8,128)S(1)}, u32[]{:S(2)}, u32[]{:S(2)}) %collective-permute-start.8) | collective-permute-done | bytes 262176 | tf_op jit(solution)/shard_map/ppermute | solution.py:17
  71.1 4.4 %collective-permute-done.9 = f32[1,32,2048]{2,1,0:T(8,128)S(1)} collective-permute-done((f32[1,32,2048]{2,1,0:T(8,128)S(1)}, f32[1,32,2048]{2,1,0:T(8,128)S(1)}, u32[]{:S(2)}, u32[]{:S(2)}) %collective-permute-start.9) | collective-permute-done | bytes 262176 | tf_op jit(solution)/shard_map/ppermute | solution.py:19
  75.5 2.0 %fusion.210 = f32[1,32,2048]{2,1,0:T(8,128)} fusion(f32[32,2048]{1,0:T(8,128)S(1)} %fusion.187, f32[1,32,2048]{2,1,0:T(8,128)S(1)} %collective-permute-done.9, f32[1,32,2048]{2,1,0:T(8,128)S(1)} %collective-permute-done.8, f32[]{:T(128)} %bitcast.1, f32[]{:T(128)} %bitcast, f32[]{:T(128)S(6)} %sub.369, pred[]{:T(512)S(6)} %eq.9, pred[]{:T(512)S(6)} %eq.8), kind=kLoop, calls=%fused_computation.325 | loop fusion | flops 458752 | bytes 1048590 | tf_op jit(solution)/shard_map/broadcast_in_dim | solution.py:58
  (141 shorter events, 15.8 us)
Async XLA Ops:
  0.0 6.4 %copy-start = (f32[1,32,2048]{2,1,0:T(8,128)S(1)}, f32[1,32,2048]{2,1,0:T(8,128)}, u32[]{:S(2)}) copy-start(f32[1,32,2048]{2,1,0:T(8,128)} %param.5) | copy-start | bytes 786436
  1.2 20.7 %collective-permute-start.2 = (f32[2,12,2048]{2,1,0:T(8,128)S(1)}, f32[2,12,2048]{2,1,0:T(8,128)S(1)}, u32[]{:S(2)}, u32[]{:S(2)}) collective-permute-start(f32[2,12,2048]{2,1,0:T(8,128)S(1)} %get-tuple-element.11), channel_id=1, source_target_pairs={{0,1},{1,2},{2,3},{3,4},{4,5},{5,6},{6,7},{7,0},{8,9},{9,10},{10,1... | collective-permute-start | bytes 589832 | tf_op jit(solution)/shard_map/ppermute | solution.py:17
  3.3 18.6 %collective-permute-start.3 = (f32[2,12,2048]{2,1,0:T(8,128)S(1)}, f32[2,12,2048]{2,1,0:T(8,128)S(1)}, u32[]{:S(2)}, u32[]{:S(2)}) collective-permute-start(f32[2,12,2048]{2,1,0:T(8,128)S(1)} %get-tuple-element.12), channel_id=1, source_target_pairs={{1,0},{2,1},{3,2},{4,3},{5,4},{6,5},{7,6},{0,7},{9,8},{10,9},{11,1... | collective-permute-start | bytes 589832 | tf_op jit(solution)/shard_map/ppermute | solution.py:19
  6.4 4.2 %copy-start.6 = (f32[2048]{0:T(1024)S(1)}, f32[2048]{0:T(1024)}, u32[]{:S(2)}) copy-start(f32[2048]{0:T(1024)} %param.8) | copy-start | bytes 24580
  6.4 13.1 %collective-permute-start = (f32[12,2048]{1,0:T(8,128)S(1)}, f32[12,2048]{1,0:T(8,128)S(1)}, u32[]{:S(2)}, u32[]{:S(2)}) collective-permute-start(f32[12,2048]{1,0:T(8,128)S(1)} %get-tuple-element.203), channel_id=1, source_target_pairs={{0,1},{1,2},{2,3},{3,4},{4,5},{5,6},{6,7},{7,0},{8,9},{9,10},{10,1... | collective-permute-start | bytes 294920 | tf_op jit(solution)/shard_map/ppermute | solution.py:17
  6.5 14.9 %collective-permute-start.1 = (f32[12,2048]{1,0:T(8,128)S(1)}, f32[12,2048]{1,0:T(8,128)S(1)}, u32[]{:S(2)}, u32[]{:S(2)}) collective-permute-start(f32[12,2048]{1,0:T(8,128)S(1)} %get-tuple-element.204), channel_id=1, source_target_pairs={{1,0},{2,1},{3,2},{4,3},{5,4},{6,5},{7,6},{0,7},{9,8},{10,9},{11,1... | collective-permute-start | bytes 294920 | tf_op jit(solution)/shard_map/ppermute | solution.py:19
  19.5 2.3 %copy-start.3 = (f32[12,2048]{1,0:T(8,128)}, f32[12,2048]{1,0:T(8,128)S(1)}, u32[]{:S(2)}) copy-start(f32[12,2048]{1,0:T(8,128)S(1)} %collective-permute-done) | copy-start | bytes 294916
  21.6 1.0 %copy-start.1 = (f32[32,2048]{1,0:T(8,128)S(1)}, f32[32,2048]{1,0:T(8,128)}, u32[]{:S(2)}) copy-start(f32[32,2048]{1,0:T(8,128)} %param.6) | copy-start | bytes 786436
  21.6 1.0 %copy-start.2 = (f32[32,2048]{1,0:T(8,128)S(1)}, f32[32,2048]{1,0:T(8,128)}, u32[]{:S(2)}) copy-start(f32[32,2048]{1,0:T(8,128)} %param.7) | copy-start | bytes 786436
  21.9 0.9 %copy-start.4 = (f32[12,2048]{1,0:T(8,128)S(1)}, f32[12,2048]{1,0:T(8,128)}, u32[]{:S(2)}) copy-start(f32[12,2048]{1,0:T(8,128)} %copy-done.3) | copy-start | bytes 294916
  22.7 0.7 slice-start
  32.9 9.2 %collective-permute-start.4 = (f32[1,32,2048]{2,1,0:T(8,128)S(1)}, f32[1,32,2048]{2,1,0:T(8,128)S(1)}, u32[]{:S(2)}, u32[]{:S(2)}) collective-permute-start(f32[1,32,2048]{2,1,0:T(8,128)S(1)} %bitcast.145), channel_id=1, source_target_pairs={{0,8},{8,16},{16,24},{1,9},{9,17},{17,25},{2,10},{10,18},{18,26},{... | collective-permute-start | bytes 786440 | tf_op jit(solution)/shard_map/ppermute | solution.py:17
  37.7 7.7 %collective-permute-start.5 = (f32[1,32,2048]{2,1,0:T(8,128)S(1)}, f32[1,32,2048]{2,1,0:T(8,128)S(1)}, u32[]{:S(2)}, u32[]{:S(2)}) collective-permute-start(f32[1,32,2048]{2,1,0:T(8,128)S(1)} %bitcast.146), channel_id=1, source_target_pairs={{8,0},{16,8},{24,16},{9,1},{17,9},{25,17},{10,2},{18,10},{26,18},{... | collective-permute-start | bytes 786440 | tf_op jit(solution)/shard_map/ppermute | solution.py:19
  39.6 0.7 copy-start.7
  46.7 6.6 %collective-permute-start.6 = (f32[12,2048]{1,0:T(8,128)S(1)}, f32[12,2048]{1,0:T(8,128)S(1)}, u32[]{:S(2)}, u32[]{:S(2)}) collective-permute-start(f32[12,2048]{1,0:T(8,128)S(1)} %get-tuple-element.201), channel_id=1, source_target_pairs={{0,1},{1,2},{2,3},{3,4},{4,5},{5,6},{6,7},{7,0},{8,9},{9,10},{10,1... | collective-permute-start | bytes 294920 | tf_op jit(solution)/shard_map/ppermute | solution.py:17
  47.1 6.2 %collective-permute-start.7 = (f32[12,2048]{1,0:T(8,128)S(1)}, f32[12,2048]{1,0:T(8,128)S(1)}, u32[]{:S(2)}, u32[]{:S(2)}) collective-permute-start(f32[12,2048]{1,0:T(8,128)S(1)} %get-tuple-element.202), channel_id=1, source_target_pairs={{1,0},{2,1},{3,2},{4,3},{5,4},{6,5},{7,6},{0,7},{9,8},{10,9},{11,1... | collective-permute-start | bytes 294920 | tf_op jit(solution)/shard_map/ppermute | solution.py:19
  53.3 0.7 copy-start.5
  53.9 0.7 slice-start.1
  64.9 6.2 %collective-permute-start.8 = (f32[1,32,2048]{2,1,0:T(8,128)S(1)}, f32[1,32,2048]{2,1,0:T(8,128)S(1)}, u32[]{:S(2)}, u32[]{:S(2)}) collective-permute-start(f32[1,32,2048]{2,1,0:T(8,128)S(1)} %bitcast.147), channel_id=1, source_target_pairs={{0,8},{8,16},{16,24},{1,9},{9,17},{17,25},{2,10},{10,18},{18,26},{... | collective-permute-start | bytes 786440 | tf_op jit(solution)/shard_map/ppermute | solution.py:17
  67.9 7.7 %collective-permute-start.9 = (f32[1,32,2048]{2,1,0:T(8,128)S(1)}, f32[1,32,2048]{2,1,0:T(8,128)S(1)}, u32[]{:S(2)}, u32[]{:S(2)}) collective-permute-start(f32[1,32,2048]{2,1,0:T(8,128)S(1)} %bitcast.148), channel_id=1, source_target_pairs={{8,0},{16,8},{24,16},{9,1},{17,9},{25,17},{10,2},{18,10},{26,18},{... | collective-permute-start | bytes 786440 | tf_op jit(solution)/shard_map/ppermute | solution.py:19
where the time goes:
time: 77.9 us; the launch traced here: 77.5 us
  starting transfers between devices  25.2 us (32%)
  waiting for transfers between devices  22.2 us (28%)
  other arithmetic  16.5 us (21%)
  local copies, waits for them, and re-layouts  11.8 us (15%)
  between operations  1.81 us (2%)
    ppermute x5, starting transfers between devices, with_halo(): lax.ppermute(head, axis, [((i + 1) % count, i) for i in range(ends)])  15 us
    ppermute x5, waiting for transfers between devices, with_halo(): lax.ppermute(tail, axis, [(i, (i + 1) % count) for i in range(ends)])  12.6 us
    sub x22, other arithmetic, advance(): field + 0.1 * mobility * (laplace + field - field * field * field + tilt)  10.4 us
    ppermute x5, starting transfers between devices, with_halo(): lax.ppermute(tail, axis, [(i, (i + 1) % count) for i in range(ends)])  10.2 us
    ppermute x5, waiting for transfers between devices, with_halo(): lax.ppermute(head, axis, [((i + 1) % count, i) for i in range(ends)])  9.61 us
    slice x48, local copies, waits for them, and re-layouts, advance(): horizontal = jnp.roll(field, 1, -1) + jnp.roll(field, -1, -1)  6.24 us
    broadcast_in_dim x1, other arithmetic, body(): return field[None]  1.99 us
    slice x48, local copies, waits for them, and re-layouts, advance(): below = jnp.roll(field, 1, -2)  1.95 us
  transfers between devices with their start and end apart: 10, of which 6 were waited for; matrix products, arithmetic and copies ran while one was open for 1% of the time, Pallas kernels for 0%

commit v1 on v0

v1 whole, which is shorter than its diff:
```python
import functools

import jax
import jax.numpy as jnp
from jax import lax
from jax.experimental import pallas as pl
from jax.experimental.pallas import tpu as pltpu
from jax.sharding import PartitionSpec as P

CYCLES = 2
DEPTH = 12
LANES = 128
SUBS = 8
CHUNK = 4
MESH = pl.DeviceIdType.MESH


def kernel(sizes, init_hbm, mob_hbm, tilt_hbm, drift_ref, mix_ref, out_hbm,
           stage, coef, fields, beside, ostage, load_sem, send_sem, recv_sem):
    n_ladder, n_space, height, halves, blocks = sizes
    place = lax.axis_index("ladder")
    slab = lax.axis_index("space")
    prev = lax.rem(slab + n_space - 1, n_space)
    following = lax.rem(slab + 1, n_space)
    core = lax.rem(place, 2)
    partner = place + 1 - 2 * core
    has_lower = place > 0
    has_upper = place < n_ladder - 1
    top, bottom = DEPTH, DEPTH + height
    full = height + 2 * DEPTH

    sources = (mob_hbm, tilt_hbm, init_hbm.at[0])
    loads = []
    for a, src in enumerate(sources):
        for j in range(blocks):
            copy = pltpu.make_async_copy(
                src.at[:, pl.ds(j * LANES, LANES)],
                stage.at[a, pl.ds(j * height, height), :],
                load_sem.at[a, j],
            )
            copy.start()
            loads.append(copy)

    barrier = pltpu.get_barrier_semaphore()
    for target in (prev, following):
        pl.semaphore_signal(barrier, inc=1, device_id={"space": target}, device_id_type=MESH)

    for target in (lax.rem(place + n_ladder - 1, n_ladder), lax.rem(place + 1, n_ladder)):
        pl.semaphore_signal(barrier, inc=1, device_id={"ladder": target}, device_id_type=MESH)

    def remote(index, src, dst, device):
        return pltpu.make_async_remote_copy(
            src_ref=src, dst_ref=dst, send_sem=send_sem.at[index], recv_sem=recv_sem.at[index],
            device_id=device, device_id_type=MESH)

    def spread(a, dst, scale):
        for r in range(height):
            for v in range(halves):
                tile = stage[a, pl.ds(v * height + r, SUBS, stride=halves * height), :]
                dst[top + r, v] = tile * scale if scale is not None else tile

    wide = DEPTH - 1
    for copy in loads[: 2 * blocks]:
        copy.wait()
    spread(0, coef.at[0], 0.1)
    spread(1, coef.at[1], None)

    pl.semaphore_wait(barrier, 4)

    coef_up = remote(0, coef.at[core, pl.ds(top, wide)], coef.at[core, pl.ds(bottom, wide)], {"space": prev})
    coef_down = remote(1, coef.at[core, pl.ds(bottom - wide, wide)], coef.at[core, pl.ds(1, wide)], {"space": following})
    coef_up.start()
    coef_down.start()
    for copy in loads[2 * blocks:]:
        copy.wait()
    spread(2, fields.at[0], None)

    def halo(index, f):
        up = remote(index, f.at[pl.ds(top, DEPTH)], f.at[pl.ds(bottom, DEPTH)], {"space": prev})
        down = remote(index + 1, f.at[pl.ds(bottom - DEPTH, DEPTH)], f.at[pl.ds(0, DEPTH)], {"space": following})
        return up, down

    halo_up, halo_down = halo(2, fields.at[0])
    halo_up.start()
    halo_down.start()

    lane = lax.broadcasted_iota(jnp.int32, (SUBS, LANES), 1)
    at_first = lane == 0
    at_last = lane == LANES - 1
    drifts = [drift_ref[pl.ds(v, SUBS, stride=halves), :] for v in range(halves)]
    speeds = [jnp.abs(u) for u in drifts]
    rises = [u > 0.0 for u in drifts]

    def rows(src, dst, lo, count):
        for first in range(0, count, CHUNK):
            many = min(CHUNK, count - first)
            base = lo + first
            tiles = [[src[base - 1 + r, v] for v in range(halves)] for r in range(many + 2)]
            for r in range(many):
                below, here, above = tiles[r], tiles[r + 1], tiles[r + 2]
                right = [pltpu.roll(here[v], 1, 1) for v in range(halves)]
                left = [pltpu.roll(here[v], LANES - 1, 1) for v in range(halves)]
                before = [pltpu.roll(right[-1], 1, 0)] + right[:-1]
                after = left[1:] + [pltpu.roll(left[0], SUBS - 1, 0)]
                for v in range(halves):
                    p = here[v]
                    side = jnp.where(at_first, before[v], right[v]) + jnp.where(at_last, after[v], left[v])
                    around = side + (below[v] + above[v]) + coef[1, base + r, v]
                    drive = around - p * (p * p + 3.0)
                    carried = jnp.where(rises[v], below[v], above[v]) - p
                    dst[base + r, v] = p + speeds[v] * carried + coef[0, base + r, v] * drive

    def level(cycle, k):
        return fields.at[3 * cycle + (0 if k == 0 else 1 + (k + 1) % 2)]

    def pyramid(cycle):
        for k in range(1, DEPTH + 1):
            rows(level(cycle, k - 1), level(cycle, k), top + k, height - 2 * k)

    def rim(cycle, start, step):
        rows(level(cycle, 0), level(cycle, 1), start + step, DEPTH)

        def two(j, carry):
            at = start + step * (2 * j + 2)
            rows(level(cycle, 1), level(cycle, 2), at, DEPTH)
            rows(level(cycle, 2), level(cycle, 1), at + step, DEPTH)
            return carry
        lax.fori_loop(0, DEPTH // 2 - 1, two, 0)
        rows(level(cycle, 1), level(cycle, 2), start + step * DEPTH, DEPTH)

    def upper_rim(cycle):
        rim(cycle, 0, 1)

    def lower_rim(cycle):
        rim(cycle, bottom, -1)

    pieces = ((DEPTH, height - 2 * DEPTH), (0, DEPTH), (height - DEPTH, DEPTH))

    def mixing(cycle, piece, action):
        start, count = pieces[piece]
        mine = fields.at[3 * cycle + 2, pl.ds(top + start, count)]
        index = 6 + 8 * cycle + 2 * piece
        for side, (exists, shift) in enumerate(((has_lower, -1), (has_upper, 1))):
            @pl.when(exists)
            def _():
                copy = remote(index + side, mine, beside.at[cycle, 1 - side, pl.ds(start, count)], {"ladder": place + shift})
                if action == "start":
                    copy.start()
                elif action == "sent":
                    copy.wait_send()

    def arrive(cycle, piece):
        start, count = pieces[piece]
        index = 6 + 8 * cycle + 2 * piece
        for side, exists in enumerate((has_lower, has_upper)):
            @pl.when(exists)
            def _():
                spot = beside.at[cycle, side, pl.ds(start, count)]
                remote(index + 1 - side, spot, spot, {"ladder": place + (2 * side - 1)}).wait_recv()

    lower_w = mix_ref[0, 0]
    upper_w = mix_ref[0, 1]
    own_w = 1.0 - lower_w - upper_w

    def mixed(cycle, piece, put):
        start, count = pieces[piece]
        for r in range(start, start + count):
            for v in range(halves):
                p = fields[3 * cycle + 2, top + r, v]
                lower = jnp.where(has_lower, beside[cycle, 0, r, v], p)
                upper = jnp.where(has_upper, beside[cycle, 1, r, v], p)
                put(r, v, own_w * p + lower_w * lower + upper_w * upper)

    def next_field(r, v, value):
        fields[3, top + r, v] = value

    def output(r, v, value):
        ostage[pl.ds(v * height + r, SUBS, stride=halves * height), :] = value

    pyramid(0)
    mixing(0, 0, "start")
    coef_up.wait_recv()
    pass_up = remote(4, coef.at[core, pl.ds(bottom, wide)], coef.at[core, pl.ds(bottom, wide)], {"ladder": partner})
    pass_up.start()
    coef_down.wait_recv()
    pass_down = remote(5, coef.at[core, pl.ds(1, wide)], coef.at[core, pl.ds(1, wide)], {"ladder": partner})
    pass_down.start()
    halo_down.wait_recv()
    pass_down.wait_recv()
    upper_rim(0)
    mixing(0, 1, "start")
    halo_up.wait_recv()
    pass_up.wait_recv()
    lower_rim(0)
    mixing(0, 2, "start")
    next_up, next_down = halo(12, fields.at[3])
    arrive(0, 1)
    mixed(0, 1, next_field)
    next_up.start()
    arrive(0, 2)
    mixed(0, 2, next_field)
    next_down.start()
    arrive(0, 0)
    mixed(0, 0, next_field)

    pyramid(1)
    mixing(1, 0, "start")
    next_down.wait_recv()
    upper_rim(1)
    mixing(1, 1, "start")
    next_up.wait_recv()
    lower_rim(1)
    mixing(1, 2, "start")
    for piece in range(3):
        arrive(1, piece)
        mixed(1, piece, output)
    stores = []
    for j in range(blocks):
        copy = pltpu.make_async_copy(
            ostage.at[pl.ds(j * height, height), :],
            out_hbm.at[0, :, pl.ds(j * LANES, LANES)],
            load_sem.at[0, j],
        )
        copy.start()
        stores.append(copy)
    for copy in (coef_up, coef_down, halo_up, halo_down, pass_up, pass_down, next_up, next_down):
        copy.wait_send()
    for cycle in range(CYCLES):
        for piece in range(3):
            mixing(cycle, piece, "sent")
    for copy in stores:
        copy.wait()


def body(initial, mobility, tilt, drift, mix_weights):
    n_ladder = lax.axis_size("ladder")
    n_space = lax.axis_size("space")
    _, height, cols = initial.shape
    blocks = cols // LANES
    halves = blocks // SUBS
    full = height + 2 * DEPTH
    f32 = jnp.float32
    hbm = pl.BlockSpec(memory_space=pl.ANY)
    return pl.pallas_call(
        functools.partial(kernel, (n_ladder, n_space, height, halves, blocks)),
        out_shape=jax.ShapeDtypeStruct(initial.shape, f32),
        in_specs=[hbm, hbm, hbm, pl.BlockSpec(memory_space=pltpu.VMEM), pl.BlockSpec(memory_space=pltpu.SMEM)],
        out_specs=hbm,
        scratch_shapes=[
            pltpu.VMEM((3, blocks * height, LANES), f32),
            pltpu.VMEM((2, full, halves, SUBS, LANES), f32),
            pltpu.VMEM((3 * CYCLES, full, halves, SUBS, LANES), f32),
            pltpu.VMEM((CYCLES, 2, height, halves, SUBS, LANES), f32),
            pltpu.VMEM((blocks * height, LANES), f32),
            pltpu.SemaphoreType.DMA((3, blocks)),
            pltpu.SemaphoreType.DMA((20,)),
            pltpu.SemaphoreType.DMA((20,)),
        ],
        compiler_params=pltpu.CompilerParams(collective_id=0, has_side_effects=True),
    )(initial, mobility, tilt, drift.reshape(blocks, LANES), mix_weights)


def solution(mesh):
    in_specs = (
        P("ladder", "space", None),
        P("space", None),
        P("space", None),
        P(),
        P("ladder", None),
    )
    out_specs = P("ladder", "space", None)
    return jax.shard_map(body, mesh=mesh, in_specs=in_specs, out_specs=out_specs, check_vma=False)
```

time: 77.9 us -> 38.4 us (0.49)
  Pallas kernels: 0 us -> 36.5 us
  starting transfers between devices: 25.2 us -> 0 us
  waiting for transfers between devices: 22.2 us -> 0 us
  other arithmetic: 16.5 us -> 0 us
  local copies, waits for them, and re-layouts: 11.8 us -> 1.67 us
  between operations: 1.81 us -> 0.01 us
    pallas_call x0 -> x1, Pallas kernels: none -> 36.5 us  [body(): pl.pallas_call(functools.partial(kernel, (n_ladder, n_space, height, halv...]
    ppermute x10 -> x0, starting transfers between devices: 25.2 us -> none  [the longest x5 15 us: with_halo(): lax.ppermute(head, axis, [((i + 1) % count, i) for i in range(ends)])]
    ppermute x10 -> x0, waiting for transfers between devices: 22.2 us -> none  [the longest x5 12.6 us: with_halo(): lax.ppermute(tail, axis, [(i, (i + 1) % count) for i in range(ends)])]
    sub x24 -> x0, other arithmetic: 10.9 us -> none  [the longest x22 10.4 us: advance(): field + 0.1 * mobility * (laplace + field - field * field * field + tilt)]
    slice x103 -> x0, local copies, waits for them, and re-layouts: 10.1 us -> none  [the longest x48 6.24 us: advance(): horizontal = jnp.roll(field, 1, -1) + jnp.roll(field, -1, -1)]
    broadcast_in_dim x1 -> x0, other arithmetic: 1.99 us -> none  [body(): return field[None]]
    add x1 -> x0, other arithmetic: 1.28 us -> none  [body(): (1.0 - lower_w - upper_w) * field + lower_w * lower + upper_w * upper]
    another operation x1 -> x0, other arithmetic: 1.17 us -> none  [body(): jnp.stack([mobility, tilt])]
  transfers between devices with their start and end apart: 10 -> 0, of which waited for: 6 -> 0; matrix products, arithmetic and copies ran while one was open for 1% -> 0% of each run, Pallas kernels for 0% -> 0%
where the time goes in v1:
time: 38.4 us; the launch traced here: 38.2 us
  Pallas kernels  36.5 us (95%)
  local copies, waits for them, and re-layouts  1.67 us (4%)
    pallas_call x1, Pallas kernels, body(): pl.pallas_call(functools.partial(kernel, (n_ladder, n_space, height, halv...  36.5 us
    unnamed x1, local copies, waits for them, and re-layouts  1.67 us

profile of v1, /device:TPU:1, one launch (start us, length us, event | category | flops | bytes accessed | tf_op | source)
XLA Modules:
  0.0 38.2 jit_solution(3104900637521037228)
XLA Ops:
  0.0 36.5 %shard_map.55 = f32[1,32,2048]{2,1,0:T(8,128)} custom-call(f32[1,32,2048]{2,1,0:T(8,128)} %init_hbm.1, f32[32,2048]{1,0:T(8,128)} %mob_hbm.1, f32[32,2048]{1,0:T(8,128)} %tilt_hbm.1, f32[16,128]{1,0:T(8,128)} %bitcast.1, f32[1,2]{1,0:T(1,128)} %mix_ref.1), custom_call_target="tpu_custom_call" | custom-call | tf_op jit(solution)/shard_map/pallas_call | solution.py:244
  36.5 1.7 %copy.7 = f32[1,32,2048]{2,1,0:T(8,128)} copy(f32[1,32,2048]{2,1,0:T(8,128)} %shard_map.55) | data formatting | bytes 524288

commit v2 on v1

v2 whole, which is shorter than its diff:
```python
import functools

import jax
import jax.numpy as jnp
from jax import lax
from jax.experimental import pallas as pl
from jax.experimental.pallas import tpu as pltpu
from jax.sharding import PartitionSpec as P

CYCLES = 2
DEPTH = 12
LANES = 128
SUBS = 8
STRIP = 4
BLOCK = 4
MESH = pl.DeviceIdType.MESH


def kernel(sizes, init_hbm, mob_hbm, tilt_hbm, drift_ref, mix_ref, out_hbm,
           stage, coef, fields, beside, ostage, load_sem, send_sem, recv_sem):
    n_ladder, n_space, height, halves, blocks = sizes
    place = lax.axis_index("ladder")
    slab = lax.axis_index("space")
    prev = lax.rem(slab + n_space - 1, n_space)
    following = lax.rem(slab + 1, n_space)
    strips = DEPTH // STRIP
    group = 4 if n_ladder % 4 == 0 else 2
    member = lax.rem(place, group)
    has_lower = place > 0
    has_upper = place < n_ladder - 1
    top, bottom = DEPTH, DEPTH + height

    sources = (mob_hbm, tilt_hbm, init_hbm.at[0])
    loads = []
    for a, src in enumerate(sources):
        for j in range(blocks):
            copy = pltpu.make_async_copy(
                src.at[:, pl.ds(j * LANES, LANES)],
                stage.at[a, pl.ds(j * height, height), :],
                load_sem.at[a, j],
            )
            copy.start()
            loads.append(copy)

    barrier = pltpu.get_barrier_semaphore()
    for target in (prev, following):
        pl.semaphore_signal(barrier, inc=1, device_id={"space": target}, device_id_type=MESH)

    around_me = [lax.rem(place + n_ladder - 1, n_ladder), lax.rem(place + 1, n_ladder)]
    around_me += [place - member + lax.rem(member + hop, group) for hop in range(1, group)]
    for target in around_me:
        pl.semaphore_signal(barrier, inc=1, device_id={"ladder": target}, device_id_type=MESH)

    def remote(index, src, dst, device):
        return pltpu.make_async_remote_copy(
            src_ref=src, dst_ref=dst, send_sem=send_sem.at[index], recv_sem=recv_sem.at[index],
            device_id=device, device_id_type=MESH)

    def spread(a, dst, scale):
        for r in range(height):
            for v in range(halves):
                tile = stage[a, pl.ds(v * height + r, SUBS, stride=halves * height), :]
                dst[top + r, v] = tile * scale if scale is not None else tile

    for copy in loads[: 2 * blocks]:
        copy.wait()
    spread(0, coef.at[0], 0.1)
    spread(1, coef.at[1], None)

    pl.semaphore_wait(barrier, 2 + len(around_me))

    kind = lax.rem(member, 2)
    share = 2 * DEPTH // group
    offset = lax.div(member, 2) * share
    near_top = coef.at[kind, pl.ds(top + offset, share)]
    near_bottom = coef.at[kind, pl.ds(bottom - DEPTH + offset, share)]
    far_top = coef.at[kind, pl.ds(offset, share)]
    far_bottom = coef.at[kind, pl.ds(bottom + offset, share)]
    coef_up = remote(0, near_top, far_bottom, {"space": prev})
    coef_down = remote(1, near_bottom, far_top, {"space": following})
    coef_up.start()
    coef_down.start()
    for copy in loads[2 * blocks:]:
        copy.wait()
    spread(2, fields.at[0], None)

    def halo(cycle, t):
        f = fields.at[3 * cycle]
        near = t * STRIP
        far = DEPTH - STRIP - t * STRIP
        index = 2 + 6 * cycle + 2 * t
        up = remote(index, f.at[pl.ds(top + near, STRIP)], f.at[pl.ds(bottom + near, STRIP)], {"space": prev})
        down = remote(index + 1, f.at[pl.ds(bottom - STRIP - near, STRIP)], f.at[pl.ds(far, STRIP)], {"space": following})
        return up, down

    halos = [[halo(cycle, t) for t in range(strips)] for cycle in range(CYCLES)]
    for t in range(strips):
        for copy in halos[0][t]:
            copy.start()

    passes = []
    for hop in range(1, group):
        other = {"ladder": place - member + lax.rem(member + hop, group)}
        index = 14 + 2 * (hop - 1)
        passes.append((remote(index, far_bottom, far_bottom, other), remote(index + 1, far_top, far_top, other)))

    lane = lax.broadcasted_iota(jnp.int32, (SUBS, LANES), 1)
    at_first = lane == 0
    at_last = lane == LANES - 1
    drifts = [drift_ref[pl.ds(v, SUBS, stride=halves), :] for v in range(halves)]
    speeds = [jnp.abs(u) for u in drifts]
    rises = [u > 0.0 for u in drifts]

    def rows(src, dst, base, many=STRIP):
        tiles = [[src[base - 1 + r, v] for v in range(halves)] for r in range(many + 2)]
        for r in range(many):
            below, here, above = tiles[r], tiles[r + 1], tiles[r + 2]
            right = [pltpu.roll(here[v], 1, 1) for v in range(halves)]
            left = [pltpu.roll(here[v], LANES - 1, 1) for v in range(halves)]
            before = [pltpu.roll(right[-1], 1, 0)] + right[:-1]
            after = left[1:] + [pltpu.roll(left[0], SUBS - 1, 0)]
            for v in range(halves):
                p = here[v]
                side = jnp.where(at_first, before[v], right[v]) + jnp.where(at_last, after[v], left[v])
                around = side + (below[v] + above[v]) + coef[1, base + r, v]
                drive = around - p * (p * p + 3.0)
                carried = jnp.where(rises[v], below[v], above[v]) - p
                dst[base + r, v] = p + speeds[v] * carried + coef[0, base + r, v] * drive

    def level(cycle, k):
        return fields.at[3 * cycle + (0 if k == 0 else 1 + (k + 1) % 2)]

    def pyramid(cycle):
        for k in range(1, DEPTH + 1):
            src, dst = level(cycle, k - 1), level(cycle, k)
            count = height - 2 * k
            start = top + k

            def some(c, carry):
                rows(src, dst, start + c * BLOCK, BLOCK)
                return carry
            lax.fori_loop(0, count // BLOCK, some, 0)
            if count % BLOCK:
                rows(src, dst, start + count - count % BLOCK, count % BLOCK)

    def strip(cycle, t):
        low = DEPTH - STRIP - t * STRIP
        high = bottom + t * STRIP

        def both(src, dst, k):
            rows(src, dst, low + k)
            rows(src, dst, high - k)

        both(level(cycle, 0), level(cycle, 1), 1)

        def two(j, carry):
            both(level(cycle, 1), level(cycle, 2), 2 * j + 2)
            both(level(cycle, 2), level(cycle, 1), 2 * j + 3)
            return carry
        lax.fori_loop(0, DEPTH // 2 - 1, two, 0)
        both(level(cycle, 1), level(cycle, 2), DEPTH)

    inner = DEPTH - STRIP
    pieces = [[(inner, height - 2 * inner)]]
    for t in range(1, strips):
        pieces.append([(inner - t * STRIP, STRIP), (height - inner + (t - 1) * STRIP, STRIP)])
    numbers = {}
    for cycle in range(CYCLES):
        for piece in [p for group_of in pieces for p in group_of]:
            numbers[cycle, piece] = 14 + 2 * (group - 1) + 2 * len(numbers)

    def mixing(cycle, piece, action):
        start, count = piece
        mine = fields.at[3 * cycle + 2, pl.ds(top + start, count)]
        index = numbers[cycle, piece]
        for side, (exists, shift) in enumerate(((has_lower, -1), (has_upper, 1))):
            @pl.when(exists)
            def _():
                copy = remote(index + side, mine, beside.at[cycle, 1 - side, pl.ds(start, count)], {"ladder": place + shift})
                if action == "start":
                    copy.start()
                elif action == "sent":
                    copy.wait_send()

    def arrive(cycle, piece):
        start, count = piece
        index = numbers[cycle, piece]
        for side, exists in enumerate((has_lower, has_upper)):
            @pl.when(exists)
            def _():
                spot = beside.at[cycle, side, pl.ds(start, count)]
                remote(index + 1 - side, spot, spot, {"ladder": place + (2 * side - 1)}).wait_recv()

    lower_w = mix_ref[0, 0]
    upper_w = mix_ref[0, 1]
    own_w = 1.0 - lower_w - upper_w

    def mixed(cycle, piece, put):
        start, count = piece
        for r in range(start, start + count):
            for v in range(halves):
                p = fields[3 * cycle + 2, top + r, v]
                lower = jnp.where(has_lower, beside[cycle, 0, r, v], p)
                upper = jnp.where(has_upper, beside[cycle, 1, r, v], p)
                put(r, v, own_w * p + lower_w * lower + upper_w * upper)

    def next_field(r, v, value):
        fields[3, top + r, v] = value

    def output(r, v, value):
        ostage[pl.ds(v * height + r, SUBS, stride=halves * height), :] = value

    def strips_of(cycle):
        for t in range(strips):
            for copy in halos[cycle][t]:
                copy.wait_recv()
            if cycle == 0 and t == 0:
                for up, down in passes:
                    up.wait_recv()
                    down.wait_recv()
            strip(cycle, t)
            for piece in pieces[t]:
                mixing(cycle, piece, "start")

    pyramid(0)
    coef_up.wait_recv()
    for up, down in passes:
        up.start()
    coef_down.wait_recv()
    for up, down in passes:
        down.start()
    strips_of(0)
    for t in range(strips):
        for piece in pieces[t]:
            arrive(0, piece)
            mixed(0, piece, next_field)
        for copy in halos[1][strips - 1 - t]:
            copy.start()

    pyramid(1)
    strips_of(1)
    for t in range(strips):
        for piece in pieces[t]:
            arrive(1, piece)
            mixed(1, piece, output)
    stores = []
    for j in range(blocks):
        copy = pltpu.make_async_copy(
            ostage.at[pl.ds(j * height, height), :],
            out_hbm.at[0, :, pl.ds(j * LANES, LANES)],
            load_sem.at[0, j],
        )
        copy.start()
        stores.append(copy)
    for copy in (coef_up, coef_down):
        copy.wait_send()
    for pairs in halos + [passes]:
        for pair in pairs:
            for copy in pair:
                copy.wait_send()
    for cycle, piece in numbers:
        mixing(cycle, piece, "sent")
    for copy in stores:
        copy.wait()


def body(initial, mobility, tilt, drift, mix_weights):
    n_ladder = lax.axis_size("ladder")
    n_space = lax.axis_size("space")
    _, height, cols = initial.shape
    blocks = cols // LANES
    halves = blocks // SUBS
    full = height + 2 * DEPTH
    f32 = jnp.float32
    hbm = pl.BlockSpec(memory_space=pl.ANY)
    return pl.pallas_call(
        functools.partial(kernel, (n_ladder, n_space, height, halves, blocks)),
        out_shape=jax.ShapeDtypeStruct(initial.shape, f32),
        in_specs=[hbm, hbm, hbm, pl.BlockSpec(memory_space=pltpu.VMEM), pl.BlockSpec(memory_space=pltpu.SMEM)],
        out_specs=hbm,
        scratch_shapes=[
            pltpu.VMEM((3, blocks * height, LANES), f32),
            pltpu.VMEM((2, full, halves, SUBS, LANES), f32),
            pltpu.VMEM((3 * CYCLES, full, halves, SUBS, LANES), f32),
            pltpu.VMEM((CYCLES, 2, height, halves, SUBS, LANES), f32),
            pltpu.VMEM((blocks * height, LANES), f32),
            pltpu.SemaphoreType.DMA((3, blocks)),
            pltpu.SemaphoreType.DMA((48,)),
            pltpu.SemaphoreType.DMA((48,)),
        ],
        compiler_params=pltpu.CompilerParams(collective_id=0, has_side_effects=True),
    )(initial, mobility, tilt, drift.reshape(blocks, LANES), mix_weights)


def solution(mesh):
    in_specs = (
        P("ladder", "space", None),
        P("space", None),
        P("space", None),
        P(),
        P("ladder", None),
    )
    out_specs = P("ladder", "space", None)
    return jax.shard_map(body, mesh=mesh, in_specs=in_specs, out_specs=out_specs, check_vma=False)
```

time: 38.4 us -> 45.3 us (1.18)
  Pallas kernels: 36.5 us -> 43.4 us
    pallas_call x1, Pallas kernels: 36.5 us -> 43.4 us  [body(): pl.pallas_call(functools.partial(kernel, (n_ladder, n_space, height, halv...]
where the time goes in v2:
time: 45.3 us; the launch traced here: 45 us
  Pallas kernels  43.4 us (96%)
  local copies, waits for them, and re-layouts  1.67 us (4%)
    pallas_call x1, Pallas kernels, body(): pl.pallas_call(functools.partial(kernel, (n_ladder, n_space, height, halv...  43.4 us
    unnamed x1, local copies, waits for them, and re-layouts  1.67 us

profile of v2, /device:TPU:1, one launch (start us, length us, event | category | flops | bytes accessed | tf_op | source)
XLA Modules:
  0.0 45.0 jit_solution(5805046519675498890)
XLA Ops:
  0.0 43.4 %shard_map.55 = f32[1,32,2048]{2,1,0:T(8,128)} custom-call(f32[1,32,2048]{2,1,0:T(8,128)} %init_hbm.1, f32[32,2048]{1,0:T(8,128)} %mob_hbm.1, f32[32,2048]{1,0:T(8,128)} %tilt_hbm.1, f32[16,128]{1,0:T(8,128)} %bitcast.1, f32[1,2]{1,0:T(1,128)} %mix_ref.1), custom_call_target="tpu_custom_call" | custom-call | tf_op jit(solution)/shard_map/pallas_call | solution.py:276
  43.4 1.7 %copy.7 = f32[1,32,2048]{2,1,0:T(8,128)} copy(f32[1,32,2048]{2,1,0:T(8,128)} %shard_map.55) | data formatting | bytes 524288

commit v3 on v1

--- a/solution.py
+++ b/solution.py
@@ -27,7 +27,6 @@
     has_lower = place > 0
     has_upper = place < n_ladder - 1
     top, bottom = DEPTH, DEPTH + height
-    full = height + 2 * DEPTH
 
     sources = (mob_hbm, tilt_hbm, init_hbm.at[0])
     loads = []
@@ -117,22 +116,10 @@
         for k in range(1, DEPTH + 1):
             rows(level(cycle, k - 1), level(cycle, k), top + k, height - 2 * k)
 
-    def rim(cycle, start, step):
-        rows(level(cycle, 0), level(cycle, 1), start + step, DEPTH)
-
-        def two(j, carry):
-            at = start + step * (2 * j + 2)
-            rows(level(cycle, 1), level(cycle, 2), at, DEPTH)
-            rows(level(cycle, 2), level(cycle, 1), at + step, DEPTH)
-            return carry
-        lax.fori_loop(0, DEPTH // 2 - 1, two, 0)
-        rows(level(cycle, 1), level(cycle, 2), start + step * DEPTH, DEPTH)
-
-    def upper_rim(cycle):
-        rim(cycle, 0, 1)
-
-    def lower_rim(cycle):
-        rim(cycle, bottom, -1)
+    def rims(cycle):
+        for k in range(1, DEPTH + 1):
+            rows(level(cycle, k - 1), level(cycle, k), k, DEPTH)
+            rows(level(cycle, k - 1), level(cycle, k), bottom - k, DEPTH)
 
     pieces = ((DEPTH, height - 2 * DEPTH), (0, DEPTH), (height - DEPTH, DEPTH))
 
@@ -187,11 +174,10 @@
     pass_down.start()
     halo_down.wait_recv()
     pass_down.wait_recv()
-    upper_rim(0)
-    mixing(0, 1, "start")
     halo_up.wait_recv()
     pass_up.wait_recv()
-    lower_rim(0)
+    rims(0)
+    mixing(0, 1, "start")
     mixing(0, 2, "start")
     next_up, next_down = halo(12, fields.at[3])
     arrive(0, 1)
@@ -206,10 +192,9 @@
     pyramid(1)
     mixing(1, 0, "start")
     next_down.wait_recv()
-    upper_rim(1)
+    next_up.wait_recv()
+    rims(1)
     mixing(1, 1, "start")
-    next_up.wait_recv()
-    lower_rim(1)
     mixing(1, 2, "start")
     for piece in range(3):
         arrive(1, piece)

time: 38.4 us -> 34.5 us (0.90)
  Pallas kernels: 36.5 us -> 32.6 us
    pallas_call x1, Pallas kernels: 36.5 us -> 32.6 us  [body(): pl.pallas_call(functools.partial(kernel, (n_ladder, n_space, height, halv...]
where the time goes in v3:
time: 34.5 us; the launch traced here: 34.3 us
  Pallas kernels  32.6 us (94%)
  local copies, waits for them, and re-layouts  1.67 us (5%)
    pallas_call x1, Pallas kernels, body(): pl.pallas_call(functools.partial(kernel, (n_ladder, n_space, height, halv...  32.6 us
    unnamed x1, local copies, waits for them, and re-layouts  1.67 us

profile of v3, /device:TPU:1, one launch (start us, length us, event | category | flops | bytes accessed | tf_op | source)
XLA Modules:
  0.0 34.3 jit_solution(16926496041215564481)
XLA Ops:
  0.0 32.6 %shard_map.55 = f32[1,32,2048]{2,1,0:T(8,128)} custom-call(f32[1,32,2048]{2,1,0:T(8,128)} %init_hbm.1, f32[32,2048]{1,0:T(8,128)} %mob_hbm.1, f32[32,2048]{1,0:T(8,128)} %tilt_hbm.1, f32[16,128]{1,0:T(8,128)} %bitcast.1, f32[1,2]{1,0:T(1,128)} %mix_ref.1), custom_call_target="tpu_custom_call" | custom-call | tf_op jit(solution)/shard_map/pallas_call | solution.py:229
  32.6 1.7 %copy.7 = f32[1,32,2048]{2,1,0:T(8,128)} copy(f32[1,32,2048]{2,1,0:T(8,128)} %shard_map.55) | data formatting | bytes 524288
